TPU v7x, 32 devices: a whole 2x2x4 slice. The times are simulated.
32 devices in a mesh: orb: 4 (over y, x), grid: 8 (over z, core).
Axes of the slice: x: 2, y: 2, z: 4, core: 2. Of those that a mesh axis runs over, the one named last changes fastest.
Arguments:
- orbitals: float32 [32, 2048, 128], P('orb', 'grid'), may hold values from -6 to 6
- previous: float32 [32, 2048, 128], P('orb', 'grid'), may hold values from -6 to 6
- potential: float32 [32, 2048, 128], P('orb', 'grid'), may hold values from -3 to 3
- partners: int32 [32, 3], P(('orb', 'grid')), may hold values from 0 to 31, as said below
- offsets: int32 [32, 3, 3], P(('orb', 'grid')), may hold values from -16 to 16, as said below
Outputs:
- advanced: float32 [32, 2048, 128], P('orb', 'grid')
- exchange_force: float32 [32, 2048, 128], P('orb', 'grid')
Inputs may be any that keep to these rules, and one draw needn't show every extreme that they name: `partners`: row n names three different orbitals among n + 1 to n + 4, counted modulo 32; so every intersecting pair is listed once, by its first orbital. There are integer box corners of the orbitals with offsets[n, q, :] = corner[partners[n, q]] - corner[n]; both ends of the range occur in every draw.
All inputs are finite; a program needn't handle non-finite values.
Results may differ from a plain program's by a relative error of at most 0.0003.
Values sent between devices are 32-bit elements; how exact they have to be, the bound alone decides.
A program may use at most 128 MiB of HBM per device.

v0:
```python
import math
import jax
import jax.numpy as jnp
from jax import lax
from jax.sharding import PartitionSpec as P

B = 64
SWEEPS = 4
AHEAD = 4
coulomb_factor = 4.0 * math.pi
exact_share = 0.25
verlet_factor = 0.05
lower_edge = 0.5
upper_edge = 16.0


def from_behind(array, axis, by):
    count = lax.axis_size(axis)
    return lax.ppermute(array, axis, [(i, (i + by) % count) for i in range(count)])


def apply_operator(grid_field):
    leading = grid_field.ndim - 3
    padded = jnp.pad(grid_field, [(0, 0)] * leading + [(2, 2)] * 3)
    extent = grid_field.shape[-1]

    def displaced(axis_number, offset_cells):
        corner = [2, 2, 2]
        corner[axis_number] = 2 + offset_cells
        return padded[
            ...,
            corner[0] : corner[0] + extent,
            corner[1] : corner[1] + extent,
            corner[2] : corner[2] + extent,
        ]

    nearest = (
        displaced(0, 1)
        + displaced(0, -1)
        + displaced(1, 1)
        + displaced(1, -1)
        + displaced(2, 1)
        + displaced(2, -1)
    )
    farther = (
        displaced(0, 2)
        + displaced(0, -2)
        + displaced(1, 2)
        + displaced(1, -2)
        + displaced(2, 2)
        + displaced(2, -2)
    )
    return 7.5 * grid_field - 4.0 / 3.0 * nearest + 1.0 / 12.0 * farther


def sweep_weights():
    centre = 0.5 * (upper_edge + lower_edge)
    radius = 0.5 * (upper_edge - lower_edge)
    ratio_sigma = centre / radius
    previous_rho = 1.0 / ratio_sigma
    weights = []
    for turn_index in range(SWEEPS - 1):
        current_rho = 1.0 / (2.0 * ratio_sigma - previous_rho)
        weights.append((current_rho * previous_rho, 2.0 * current_rho / radius))
        previous_rho = current_rho
    return (centre, weights)


def solve_potential(density):
    centre, weights = sweep_weights()
    residual = coulomb_factor * density
    direction = residual / centre
    solution = jnp.zeros_like(density)
    for turn_index in range(SWEEPS):
        solution = solution + direction
        residual = residual - apply_operator(direction)
        if turn_index + 1 < SWEEPS:
            keep_weight, residual_weight = weights[turn_index]
            direction = keep_weight * direction + residual_weight * residual
    return solution


def shift_box(one_box, offset, direction_sign):
    extent = one_box.shape[0]
    reach_cells = extent // 4
    padded = jnp.pad(one_box, reach_cells)
    corner = (reach_cells + direction_sign * offset).astype(jnp.int32)
    return lax.dynamic_slice(padded, (corner[0], corner[1], corner[2]), (extent, extent, extent))


def pair_terms(own_box, partner_boxes, pair_offsets):

    def single(partner_box, offset):
        moved_box = shift_box(partner_box, offset, 1)
        potential_box = solve_potential(own_box * moved_box)
        return (potential_box * moved_box, shift_box(potential_box * own_box, offset, -1))

    own_terms, partner_terms = jax.vmap(single)(partner_boxes, pair_offsets)
    return (jnp.sum(own_terms, axis=0), partner_terms)


def build_windows(orbitals, upper_rows, count_local, steps_ahead):
    slab_count = lax.axis_size("grid")
    tail_shape = orbitals.shape[1:]
    blocks = jnp.concatenate([orbitals, upper_rows], axis=0)
    blocks = blocks.reshape((slab_count + steps_ahead, count_local) + tail_shape)
    ahead_rows = jnp.concatenate(
        [blocks[distance + 1 : distance + 1 + slab_count] for distance in range(steps_ahead)],
        axis=1,
    )
    windows = jnp.concatenate([blocks[:slab_count], ahead_rows], axis=1)
    return windows.reshape((slab_count * (count_local + AHEAD),) + tail_shape)


def fold_windows(returned, count_local, steps_ahead):
    slab_count = lax.axis_size("grid")
    tail_shape = returned.shape[1:]
    blocks = returned.reshape((slab_count, count_local + AHEAD) + tail_shape)
    ahead_rows = blocks[:, count_local:]
    summed = jnp.pad(blocks[:, :count_local], ((0, steps_ahead), (0, 0), (0, 0), (0, 0)))
    for distance in range(steps_ahead):
        ahead_part = ahead_rows[:, distance * count_local : (distance + 1) * count_local]
        summed = summed + jnp.pad(
            ahead_part, ((distance + 1, steps_ahead - distance - 1), (0, 0), (0, 0), (0, 0))
        )
    flattened = summed.reshape(((slab_count + steps_ahead) * count_local,) + tail_shape)
    kept_rows = slab_count * count_local
    spilled = from_behind(flattened[kept_rows : kept_rows + AHEAD], "orb", 1)
    return flattened[:kept_rows] + jnp.pad(spilled, ((0, kept_rows - AHEAD), (0, 0), (0, 0)))


def local(orbitals, previous, potential, partners, offsets):
    count_local = partners.shape[0]
    width_last = orbitals.shape[2]
    total_orbitals = lax.axis_size(("orb", "grid")) * count_local
    steps_ahead = -(-AHEAD // count_local)
    upper_rows = from_behind(orbitals[:AHEAD], "orb", -1)
    windows = build_windows(orbitals, upper_rows, count_local, steps_ahead)
    widened = lax.all_to_all(windows, "grid", split_axis=0, concat_axis=1, tiled=True)
    full_rows = widened.shape[1]
    extended = widened.reshape(count_local + AHEAD, B, B, B)
    own_boxes = extended[:count_local]
    first_index = lax.axis_index(("orb", "grid")) * count_local
    local_index = jnp.remainder(partners - first_index, total_orbitals)

    def per_orbital(packed):
        own_box, chosen, pair_offsets = packed
        return pair_terms(own_box, extended[chosen], pair_offsets)

    own_force, partner_force = lax.map(per_orbital, (own_boxes, local_index, offsets))
    spread = (
        jnp.zeros_like(extended)
        .at[local_index.reshape(-1)]
        .add(partner_force.reshape((-1,) + extended.shape[1:]))
    )
    kinetic = (-0.5 * apply_operator(own_boxes)).reshape(count_local, full_rows, width_last)
    all_force = jnp.concatenate([own_force + spread[:count_local], spread[count_local:]], axis=0)
    packed_all = (exact_share * all_force).reshape(count_local + AHEAD, full_rows, width_last)
    returned, restored = (
        lax.all_to_all(packed_all, "grid", split_axis=1, concat_axis=0, tiled=True),
        lax.all_to_all(kinetic, "grid", split_axis=1, concat_axis=0, tiled=True),
    )
    exchange_force = fold_windows(returned, count_local, steps_ahead)
    advanced = (
        2.0 * orbitals
        - previous
        + verlet_factor * (restored + exchange_force - potential * orbitals)
    )
    return (advanced, exchange_force)


def solution(mesh):
    in_specs = (
        P("orb", "grid", None),
        P("orb", "grid", None),
        P("orb", "grid", None),
        P(("orb", "grid"), None),
        P(("orb", "grid"), None, None),
    )
    out_specs = (P("orb", "grid", None), P("orb", "grid", None))
    return jax.shard_map(local, mesh=mesh, in_specs=in_specs, out_specs=out_specs, check_vma=False)
```

profile of v0, /device:TPU:0, one launch (start us, length us, event | category | flops | bytes accessed | tf_op | source)
XLA Modules:
  0.0 637.8 jit_solution(1939812428147759683)
XLA Ops:
  0.6 1.1 slice.280
  1.7 4.0 collective-permute-start
  5.7 1.3 constant_dynamic-update-slice_fusion.1
  7.0 1.3 bitcast_dynamic-update-slice_fusion
  8.3 8.6 %collective-permute-done = f32[4,256,128]{2,1,0:T(8,128)S(1)} collective-permute-done((f32[4,256,128]{2,1,0:T(8,128)S(1)}, f32[4,256,128]{2,1,0:T(8,128)S(1)}, u32[]{:S(2)}, u32[]{:S(2)}) %collective-permute-start) | collective-permute-done | bytes 524320 | tf_op jit(solution)/shard_map/ppermute | solution.py:19
  16.9 0.1 fusion.67
  17.0 0.1 fusion.66
  17.1 0.1 fusion.65
  17.2 0.1 fusion.64
  17.3 2.4 copy-done.2
  19.6 4.9 all-to-all-start
  24.5 0.1 copy.65
  24.6 0.1 copy.66
  24.8 0.1 copy.58
  24.9 0.1 copy.62
  25.0 116.1 %all-to-all-done = f32[40,256,128]{2,1,0:T(8,128)} async-done(((f32[40,256,128]{2,1,0:T(8,128)}), f32[40,256,128]{2,1,0:T(8,128)}, u32[]{:S(2)}, u32[]{:S(2)}) %all-to-all-start) | async-done | bytes 5242912 | tf_op jit(solution)/shard_map/all_to_all | solution.py:139
  141.1 5.5 copy.54
  146.5 1.3 slice.398
  147.8 8.5 %reshape.85 = f32[5,64,64,64]{3,2,1,0:T(8,128)} reshape(f32[5,8,256,128]{3,2,1,0:T(8,128)} %copy.54) | data formatting | bytes 10485760 | tf_op jit(solution)/shard_map/reshape | solution.py:141
  156.4 7.5 %gather_fusion = f32[3,64,64,64]{3,2,1,0:T(8,128)} fusion(f32[5,64,64,64]{3,2,1,0:T(8,128)} %reshape.85, s32[1024]{0:T(1024)S(1)} %pad_clamp_fusion), kind=kCustom, calls=%fused_computation | custom fusion | bytes 6291468 | tf_op jit(solution)/shard_map/while/body/eval_jaxpr/gather | solution.py:148
  163.9 10.5 %pad.51 = f32[3,96,96,96]{3,2,1,0:T(8,128)} pad(f32[3,64,64,64]{3,2,1,0:T(8,128)} %gather_fusion, f32[]{:T(128)} %constant.45.clone.1), padding=0_0x16_16x16_16x16_16 | pad | bytes 13762564 | tf_op jit(solution)/shard_map/while/body/eval_jaxpr/vmap(jit(_pad))/pad | solution.py:86
  174.4 3.5 broadcast.154.clone
  177.9 20.9 %while.2 = (s32[]{:T(128)}, f32[3,96,96,96]{3,2,1,0:T(8,128)}, s32[3,4]{1,0:T(4,128)S(1)}, f32[3,64,64,64]{3,2,1,0:T(8,128)}, s32[]{:T(128)}) while((s32[]{:T(128)}, f32[3,96,96,96]{3,2,1,0:T(8,128)}, s32[3,4]{1,0:T(4,128)S(1)}, f32[3,64,64,64]{3,2,1,0:T(8,128)}, s32[]{:T(128)}) %tuple.70), condition=%wide.while_cond, body=%wide.while_body.sunk | while | flops 2 | bytes 4196993 | solution.py:88
  177.9 0.7 fusion.84
  178.5 6.3 dynamic-slice_dynamic-update-slice_fusion.4
  184.8 0.7 fusion.84
  185.5 6.3 dynamic-slice_dynamic-update-slice_fusion.4
  191.8 0.7 fusion.84
  192.4 6.3 dynamic-slice_dynamic-update-slice_fusion.4
  198.7 0.3 mul.165
  199.1 6.9 %multiply_multiply_fusion = f32[3,64,64,64]{3,2,1,0:T(8,128)} fusion(f32[3,64,64,64]{3,2,1,0:T(8,128)} %get-tuple-element.30, f32[64,64,64]{2,1,0:T(8,128)S(1)} %mul.165), kind=kLoop, calls=%fused_computation.93 | loop fusion | flops 1572864 | bytes 7340032 | tf_op jit(solution)/shard_map/while/body/eval_jaxpr/vmap()/div | solution.py:72
  205.9 36.1 %multiply_add_fusion.1 = (f32[3,64,64,64]{3,2,1,0:T(8,128)}, f32[3,64,64,64]{3,2,1,0:T(8,128)}) fusion(f32[3,64,64,64]{3,2,1,0:T(8,128)} %get-tuple-element.30, f32[64,64,64]{2,1,0:T(8,128)S(1)} %mul.165, f32[3,64,64,64]{3,2,1,0:T(8,128)} %multiply_multiply_fusion), kind=kLoop, calls=%fused_computation.92 | loop fusion | flops 16515072 | bytes 13631488 | tf_op jit(solution)/shard_map/while/body/eval_jaxpr/vmap()/add | solution.py:79
  242.0 35.9 %multiply_add_fusion = (f32[3,64,64,64]{3,2,1,0:T(8,128)}, f32[3,64,64,64]{3,2,1,0:T(8,128)}) fusion(f32[3,64,64,64]{3,2,1,0:T(8,128)} %get-tuple-element.101, f32[3,64,64,64]{3,2,1,0:T(8,128)} %get-tuple-element.102), kind=kLoop, calls=%fused_computation.91 | loop fusion | flops 14942208 | bytes 12582912 | tf_op jit(solution)/shard_map/while/body/eval_jaxpr/vmap()/add | solution.py:79
  278.0 43.8 %multiply_reduce_fusion = (f32[64,64,64]{2,1,0:T(8,128)}, f32[3,64,64,64]{3,2,1,0:T(8,128)}) fusion(f32[3,64,64,64]{3,2,1,0:T(8,128)} %get-tuple-element.30, f32[3,64,64,64]{3,2,1,0:T(8,128)} %get-tuple-element.100, f32[3,64,64,64]{3,2,1,0:T(8,128)} %get-tuple-element.99, f32[3,64,64,64]{3,2,1,0:T(8,128)} %get-tuple-element.101, f32[64,64,64]{2,1,0:T(8,128)S(1)} %mul.165), kind=kLoop, calls=%fused_computation.90 | loop fusion | flops 20185088 | bytes 17825792 | tf_op jit(solution)/shard_map/while/body/eval_jaxpr/reduce_sum | solution.py:99
  321.8 6.9 %broadcast_multiply_fusion = f32[3,64,64,64]{3,2,1,0:T(8,128)} fusion(f32[3,64,64,64]{3,2,1,0:T(8,128)} %get-tuple-element.98, f32[64,64,64]{2,1,0:T(8,128)S(1)} %mul.165), kind=kLoop, calls=%fused_computation.96 | loop fusion | flops 786432 | bytes 7340032 | tf_op jit(solution)/shard_map/while/body/eval_jaxpr/vmap()/mul | solution.py:96
  328.7 10.5 %pad.55 = f32[3,96,96,96]{3,2,1,0:T(8,128)} pad(f32[3,64,64,64]{3,2,1,0:T(8,128)} %broadcast_multiply_fusion, f32[]{:T(128)} %constant.45.clone.1), padding=0_0x16_16x16_16x16_16 | pad | bytes 13762564 | tf_op jit(solution)/shard_map/while/body/eval_jaxpr/vmap(jit(_pad))/pad | solution.py:86
  339.2 3.4 broadcast.154
  342.5 20.1 %while.3 = (s32[]{:T(128)}, f32[3,96,96,96]{3,2,1,0:T(8,128)}, s32[3,4]{1,0:T(4,128)S(1)}, f32[3,64,64,64]{3,2,1,0:T(8,128)}, s32[]{:T(128)}) while((s32[]{:T(128)}, f32[3,96,96,96]{3,2,1,0:T(8,128)}, s32[3,4]{1,0:T(4,128)S(1)}, f32[3,64,64,64]{3,2,1,0:T(8,128)}, s32[]{:T(128)}) %tuple.73), condition=%wide.while_cond.1, body=%wide.while_body.1.sunk | while | flops 2 | bytes 4196993 | solution.py:88
  342.5 0.6 fusion.85
  343.1 6.1 dynamic-slice_dynamic-update-slice_fusion.5
  349.2 0.6 fusion.85
  349.8 6.1 dynamic-slice_dynamic-update-slice_fusion.5
  355.9 0.6 fusion.85
  356.6 6.1 dynamic-slice_dynamic-update-slice_fusion.5
  362.6 5.3 broadcast_in_dim.31
  368.0 11.9 %scatter_fusion = f32[5,64,64,64]{3,2,1,0:T(8,128)} fusion(f32[5,64,64,64]{3,2,1,0:T(8,128)} %broadcast_in_dim.31, s32[3]{0:T(128)S(1)} %fusion.74, f32[3,64,64,64]{3,2,1,0:T(8,128)} %get-tuple-element.38), kind=kCustom, calls=%fused_computation.1 | custom fusion | flops 786432 | bytes 9437196 | tf_op jit(solution)/shard_map/scatter-add | solution.py:154
  379.9 8.5 %slice.400 = f32[4,64,64,64]{3,2,1,0:T(8,128)} slice(f32[5,64,64,64]{3,2,1,0:T(8,128)} %scatter_fusion), slice={[1:5], [0:64], [0:64], [0:64]} | slice | bytes 8388608 | tf_op jit(solution)/shard_map/slice | solution.py:157
  388.4 2.0 slice_add_fusion
  390.4 1.3 concatenate.26
  391.8 7.3 %concatenate.27 = f32[4,2048,128]{2,1,0:T(8,128)} reshape(f32[4,64,64,64]{3,2,1,0:T(8,128)} %slice.400) | data formatting | bytes 8388608 | tf_op jit(solution)/shard_map/concatenate | solution.py:157
  399.1 2.5 maximum_multiply_fusion
  401.6 13.0 %copy.63 = f32[5,2048,128]{2,0,1:T(8,128)} copy(f32[5,2048,128]{2,1,0:T(8,128)S(1)} %maximum_multiply_fusion) | data formatting | bytes 10485760 | tf_op jit(solution)/shard_map/mul | solution.py:158
  414.6 5.0 all-to-all-start.2
  419.5 0.3 slice.290
  419.9 4.0 fusion.56
  423.8 3.4 reshape.84
  427.2 176.1 %all-to-all-done.2 = f32[5,2048,128]{2,0,1:T(8,128)} async-done(((f32[5,2048,128]{2,0,1:T(8,128)}), f32[5,2048,128]{2,0,1:T(8,128)}, u32[]{:S(2)}, u32[]{:S(2)}) %all-to-all-start.2) | async-done | bytes 5242912 | tf_op jit(solution)/shard_map/all_to_all | solution.py:160
  603.4 4.2 all-to-all-start.1
  607.6 4.4 copy.68
  612.0 0.4 fusion.81
  612.5 2.4 collective-permute-start.1
  614.9 0.3 pad_add_fusion
  615.1 19.1 %all-to-all-done.1 = f32[1,2048,128]{2,0,1:T(1,128)} async-done(((f32[1,2048,128]{2,0,1:T(1,128)}), f32[1,2048,128]{2,0,1:T(1,128)}, u32[]{:S(2)}, u32[]{:S(2)}) %all-to-all-start.1) | async-done | bytes 1048608 | tf_op jit(solution)/shard_map/all_to_all | solution.py:161
  634.2 3.6 multiply_add_fusion.2
  (26 shorter events, 0.2 us)
Async XLA Ops:
  1.7 15.2 %collective-permute-start = (f32[4,256,128]{2,1,0:T(8,128)S(1)}, f32[4,256,128]{2,1,0:T(8,128)S(1)}, u32[]{:S(2)}, u32[]{:S(2)}) collective-permute-start(f32[4,256,128]{2,1,0:T(8,128)S(1)} %slice.280), channel_id=1, source_target_pairs={{0,24},{8,0},{16,8},{24,16},{1,25},{9,1},{17,9},{25,17},{2,26},{10... | collective-permute-start | bytes 1572872 | tf_op jit(solution)/shard_map/ppermute | solution.py:19
  17.1 7.4 %copy-start.4 = (s32[1,3,3]{2,0,1:T(1,128)S(1)}, s32[1,3,3]{2,0,1:T(1,128)}, u32[]{:S(2)}) copy-start(s32[1,3,3]{2,0,1:T(1,128)} %param.9) | copy-start | bytes 112
  17.2 7.8 %copy-start.5 = (s32[1,3]{1,0:T(1,128)S(1)}, s32[1,3]{1,0:T(1,128)}, u32[]{:S(2)}) copy-start(s32[1,3]{1,0:T(1,128)} %param.8) | copy-start | bytes 40
  17.2 2.4 copy-start.2
  19.6 121.5 %all-to-all-start = ((f32[40,256,128]{2,1,0:T(8,128)}), f32[40,256,128]{2,1,0:T(8,128)}, u32[]{:S(2)}, u32[]{:S(2)}) async-start(f32[40,256,128]{2,1,0:T(8,128)} %bitcast.93), calls=%async_computation | async-start | bytes 10485760 | tf_op jit(solution)/shard_map/all_to_all | solution.py:139
  379.9 8.5 %copy-start.1 = (f32[64,64,64]{2,1,0:T(8,128)S(1)}, f32[64,64,64]{2,1,0:T(8,128)}, u32[]{:S(2)}) copy-start(f32[64,64,64]{2,1,0:T(8,128)} %get-tuple-element.97) | copy-start | bytes 3145732
  391.8 7.3 %copy-start.3 = (f32[1,2048,128]{2,1,0:T(8,128)S(1)}, f32[1,2048,128]{2,1,0:T(8,128)}, u32[]{:S(2)}) copy-start(f32[1,2048,128]{2,1,0:T(8,128)} %concatenate.26) | copy-start | bytes 3145732
  414.6 188.8 %all-to-all-start.2 = ((f32[5,2048,128]{2,0,1:T(8,128)}), f32[5,2048,128]{2,0,1:T(8,128)}, u32[]{:S(2)}, u32[]{:S(2)}) async-start(f32[5,2048,128]{2,0,1:T(8,128)} %copy.63), calls=%async_computation.2 | async-start | bytes 16777216 | tf_op jit(solution)/shard_map/all_to_all | solution.py:160
  603.4 30.8 %all-to-all-start.1 = ((f32[1,2048,128]{2,0,1:T(1,128)}), f32[1,2048,128]{2,0,1:T(1,128)}, u32[]{:S(2)}, u32[]{:S(2)}) async-start(f32[1,2048,128]{2,0,1:T(1,128)} %reshape.84), calls=%async_computation.1 | async-start | bytes 2097152 | tf_op jit(solution)/shard_map/all_to_all | solution.py:161
  612.4 21.8 %copy-start = (f32[8,256,128]{2,1,0:T(8,128)S(1)}, f32[8,256,128]{2,1,0:T(8,128)}, u32[]{:S(2)}) copy-start(f32[8,256,128]{2,1,0:T(8,128)} %param.5) | copy-start | bytes 3145732
  612.5 21.7 %collective-permute-start.1 = (f32[4,256,128]{2,1,0:T(8,128)S(1)}, f32[4,256,128]{2,1,0:T(8,128)}, u32[]{:S(2)}, u32[]{:S(2)}) collective-permute-start(f32[4,256,128]{2,1,0:T(8,128)S(1)} %add_bitcast_fusion), channel_id=1, source_target_pairs={{0,8},{8,16},{16,24},{24,0},{1,9},{9,17},{17,25},{25,1},{2,10},{10... | collective-permute-start | bytes 1572872 | tf_op jit(solution)/shard_map/ppermute | solution.py:19
where the time goes:
time: 639 us; the launch traced here: 638 us
  waiting for transfers between devices  320 us (50%)
  other arithmetic  154 us (24%)
  local copies, waits for them, and re-layouts  143 us (22%)
  starting transfers between devices  20.5 us (3%)
    all_to_all x1, waiting for transfers between devices, local(): lax.all_to_all(packed_all, 'grid', split_axis=1, concat_axis=0, tiled=True)  176 us
    all_to_all x1, waiting for transfers between devices, local(): lax.all_to_all(windows, 'grid', split_axis=0, concat_axis=1, tiled=True)  116 us
    add x2, other arithmetic, solve_potential(): direction = keep_weight * direction + residual_weight * residual  72 us
    reduce_sum x1, other arithmetic, pair_terms(): return (jnp.sum(own_terms, axis=0), partner_terms)  43.8 us
    gather x18, local copies, waits for them, and re-layouts  40.9 us
    pad x2, local copies, waits for them, and re-layouts, shift_box(): padded = jnp.pad(one_box, reach_cells)  21 us
    all_to_all x1, waiting for transfers between devices, local(): lax.all_to_all(kinetic, 'grid', split_axis=1, concat_axis=0, tiled=True)  19.1 us
    mul x1, local copies, waits for them, and re-layouts, local(): exact_share * all_force  13 us
  transfers between devices with their start and end apart: 5, of which 4 were waited for; matrix products, arithmetic and copies ran while one was open for 2% of the time, Pallas kernels for 0%

commit v1 on v0

--- a/solution.py
+++ b/solution.py
@@ -12,6 +12,30 @@
 verlet_factor = 0.05
 lower_edge = 0.5
 upper_edge = 16.0
+
+
+def in_blocks(x, dim, count):
+    lengths = x.shape
+    tiles = x.reshape(*lengths[:dim], count, lengths[dim] // count, *lengths[dim + 1 :])
+    return jnp.moveaxis(tiles, dim, 0)
+
+
+def joined_along(blocks, dim):
+    blocks = jnp.moveaxis(blocks, 0, dim)
+    shape = blocks.shape
+    return blocks.reshape(*shape[:dim], shape[dim] * shape[dim + 1], *shape[dim + 2 :])
+
+
+def exchange_directly(x, axis, split_dim, concat_dim):
+    size, here = (lax.axis_size(axis), lax.axis_index(axis))
+    pieces = in_blocks(x, split_dim, size)
+    whole = pieces
+    for step in range(1, size):
+        target, source = ((here + step) % size, (here - step) % size)
+        sent = lax.dynamic_index_in_dim(pieces, target, 0)
+        other = lax.ppermute(sent, axis, [(i, (i + step) % size) for i in range(size)])
+        whole = lax.dynamic_update_slice_in_dim(whole, other, source, axis=0)
+    return joined_along(whole, concat_dim)
 
 
 def from_behind(array, axis, by):
@@ -157,7 +181,7 @@
     all_force = jnp.concatenate([own_force + spread[:count_local], spread[count_local:]], axis=0)
     packed_all = (exact_share * all_force).reshape(count_local + AHEAD, full_rows, width_last)
     returned, restored = (
-        lax.all_to_all(packed_all, "grid", split_axis=1, concat_axis=0, tiled=True),
+        exchange_directly(packed_all, "grid", 1, 0),
         lax.all_to_all(kinetic, "grid", split_axis=1, concat_axis=0, tiled=True),
     )
     exchange_force = fold_windows(returned, count_local, steps_ahead)

time: 639 us -> 561 us (0.88)
  the two profiles are of different devices: /device:TPU:0 before, /device:TPU:9 now
where the time goes in v1:
time: 561 us; the launch traced here: 559 us
  waiting for transfers between devices  234 us (42%)
  other arithmetic  155 us (28%)
  local copies, waits for them, and re-layouts  140 us (25%)
  starting transfers between devices  29.4 us (5%)
    all_to_all x1, waiting for transfers between devices, local(): lax.all_to_all(windows, 'grid', split_axis=0, concat_axis=1, tiled=True)  113 us
    ppermute x7, waiting for transfers between devices, exchange_directly(): lax.ppermute(sent, axis, [(i, (i + step) % size) for i in range(size)])  106 us
    add x2, other arithmetic, solve_potential(): direction = keep_weight * direction + residual_weight * residual  70.8 us
    reduce_sum x1, other arithmetic, pair_terms(): return (jnp.sum(own_terms, axis=0), partner_terms)  43.3 us
    gather x18, local copies, waits for them, and re-layouts  40.5 us
    pad x2, local copies, waits for them, and re-layouts, shift_box(): padded = jnp.pad(one_box, reach_cells)  20.9 us
    ppermute x2, waiting for transfers between devices, from_behind(): lax.ppermute(array, axis, [(i, (i + by) % count) for i in range(count)])  15.4 us
    unnamed x22, local copies, waits for them, and re-layouts  12.3 us
  transfers between devices with their start and end apart: 11, of which 8 were waited for; matrix products, arithmetic and copies ran while one was open for 4% of the time, Pallas kernels for 0%

profile of v1, /device:TPU:9, one launch (start us, length us, event | category | flops | bytes accessed | tf_op | source)
XLA Modules:
  0.0 559.0 jit_solution(1174459311213709652)
XLA Ops:
  0.6 1.1 slice.280
  1.7 2.2 collective-permute-start
  3.9 1.3 constant_dynamic-update-slice_fusion.1
  5.2 1.3 bitcast_dynamic-update-slice_fusion
  6.5 8.0 %collective-permute-done = f32[4,256,128]{2,1,0:T(8,128)S(1)} collective-permute-done((f32[4,256,128]{2,1,0:T(8,128)S(1)}, f32[4,256,128]{2,1,0:T(8,128)S(1)}, u32[]{:S(2)}, u32[]{:S(2)}) %collective-permute-start) | collective-permute-done | bytes 524320 | tf_op jit(solution)/shard_map/ppermute | solution.py:43
  15.0 2.4 copy-done.2
  17.3 6.5 %all-to-all-start = ((f32[40,256,128]{2,1,0:T(8,128)}), f32[40,256,128]{2,1,0:T(8,128)}, u32[]{:S(2)}, u32[]{:S(2)}) async-start(f32[40,256,128]{2,1,0:T(8,128)} %bitcast.104), calls=%async_computation | async-start | bytes 10485760 | tf_op jit(solution)/shard_map/all_to_all | solution.py:163
  24.2 112.5 %all-to-all-done = f32[40,256,128]{2,1,0:T(8,128)} async-done(((f32[40,256,128]{2,1,0:T(8,128)}), f32[40,256,128]{2,1,0:T(8,128)}, u32[]{:S(2)}, u32[]{:S(2)}) %all-to-all-start) | async-done | bytes 5242912 | tf_op jit(solution)/shard_map/all_to_all | solution.py:163
  136.7 5.4 copy.41
  142.2 1.3 slice.398
  143.5 8.5 %reshape.89 = f32[5,64,64,64]{3,2,1,0:T(8,128)} reshape(f32[5,8,256,128]{3,2,1,0:T(8,128)} %copy.41) | data formatting | bytes 10485760 | tf_op jit(solution)/shard_map/reshape | solution.py:165
  152.0 7.5 %gather_fusion = f32[3,64,64,64]{3,2,1,0:T(8,128)} fusion(f32[5,64,64,64]{3,2,1,0:T(8,128)} %reshape.89, s32[1024]{0:T(1024)S(1)} %pad_clamp_fusion), kind=kCustom, calls=%fused_computation | custom fusion | bytes 6291468 | tf_op jit(solution)/shard_map/while/body/eval_jaxpr/gather | solution.py:172
  159.5 10.5 %pad.51 = f32[3,96,96,96]{3,2,1,0:T(8,128)} pad(f32[3,64,64,64]{3,2,1,0:T(8,128)} %gather_fusion, f32[]{:T(128)} %constant.178.clone.1), padding=0_0x16_16x16_16x16_16 | pad | bytes 13762564 | tf_op jit(solution)/shard_map/while/body/eval_jaxpr/vmap(jit(_pad))/pad | solution.py:110
  170.0 3.5 broadcast.168.clone
  173.5 20.4 %while.2 = (s32[]{:T(128)}, f32[3,96,96,96]{3,2,1,0:T(8,128)}, s32[3,4]{1,0:T(4,128)S(1)}, f32[3,64,64,64]{3,2,1,0:T(8,128)}, s32[]{:T(128)}) while((s32[]{:T(128)}, f32[3,96,96,96]{3,2,1,0:T(8,128)}, s32[3,4]{1,0:T(4,128)S(1)}, f32[3,64,64,64]{3,2,1,0:T(8,128)}, s32[]{:T(128)}) %tuple.75), condition=%wide.while_cond, body=%wide.while_body.sunk | while | flops 2 | bytes 4196993 | solution.py:112
  173.5 0.7 fusion.85
  174.2 6.2 %dynamic-slice_dynamic-update-slice_fusion.4 = f32[3,64,64,64]{3,2,1,0:T(8,128)} fusion(f32[3,64,64,64]{3,2,1,0:T(8,128)} %get-tuple-element.204, s32[]{:T(128)} %get-tuple-element.201, f32[3,96,96,96]{3,2,1,0:T(8,128)} %get-tuple-element.207, s32[]{:T(128)} %bitcast.96, s32[]{:T(128)} %bitcast.97, s32[]{:T(128)} %bitcast.98, s32[]{:T(128)} %bitcast.99), kind=kLoop, calls=%fused_computation.2.clone.1 | loop fusion | bytes 4196864 | tf_op jit(solution)/shard_map/while/body/eval_jaxpr/vmap()/gather
  180.3 0.7 fusion.85
  181.0 6.1 %dynamic-slice_dynamic-update-slice_fusion.4 = f32[3,64,64,64]{3,2,1,0:T(8,128)} fusion(f32[3,64,64,64]{3,2,1,0:T(8,128)} %get-tuple-element.204, s32[]{:T(128)} %get-tuple-element.201, f32[3,96,96,96]{3,2,1,0:T(8,128)} %get-tuple-element.207, s32[]{:T(128)} %bitcast.96, s32[]{:T(128)} %bitcast.97, s32[]{:T(128)} %bitcast.98, s32[]{:T(128)} %bitcast.99), kind=kLoop, calls=%fused_computation.2.clone.1 | loop fusion | bytes 4196864 | tf_op jit(solution)/shard_map/while/body/eval_jaxpr/vmap()/gather
  187.1 0.7 fusion.85
  187.8 6.1 %dynamic-slice_dynamic-update-slice_fusion.4 = f32[3,64,64,64]{3,2,1,0:T(8,128)} fusion(f32[3,64,64,64]{3,2,1,0:T(8,128)} %get-tuple-element.204, s32[]{:T(128)} %get-tuple-element.201, f32[3,96,96,96]{3,2,1,0:T(8,128)} %get-tuple-element.207, s32[]{:T(128)} %bitcast.96, s32[]{:T(128)} %bitcast.97, s32[]{:T(128)} %bitcast.98, s32[]{:T(128)} %bitcast.99), kind=kLoop, calls=%fused_computation.2.clone.1 | loop fusion | bytes 4196864 | tf_op jit(solution)/shard_map/while/body/eval_jaxpr/vmap()/gather
  194.2 6.9 %multiply_multiply_fusion = f32[3,64,64,64]{3,2,1,0:T(8,128)} fusion(f32[3,64,64,64]{3,2,1,0:T(8,128)} %get-tuple-element.30, f32[64,64,64]{2,1,0:T(8,128)S(1)} %mul.165), kind=kLoop, calls=%fused_computation.93 | loop fusion | flops 1572864 | bytes 7340032 | tf_op jit(solution)/shard_map/while/body/eval_jaxpr/vmap()/div | solution.py:96
  201.1 35.6 %multiply_add_fusion.1 = (f32[3,64,64,64]{3,2,1,0:T(8,128)}, f32[3,64,64,64]{3,2,1,0:T(8,128)}) fusion(f32[3,64,64,64]{3,2,1,0:T(8,128)} %get-tuple-element.30, f32[64,64,64]{2,1,0:T(8,128)S(1)} %mul.165, f32[3,64,64,64]{3,2,1,0:T(8,128)} %multiply_multiply_fusion), kind=kLoop, calls=%fused_computation.92 | loop fusion | flops 16515072 | bytes 13631488 | tf_op jit(solution)/shard_map/while/body/eval_jaxpr/vmap()/add | solution.py:103
  236.7 35.2 %multiply_add_fusion = (f32[3,64,64,64]{3,2,1,0:T(8,128)}, f32[3,64,64,64]{3,2,1,0:T(8,128)}) fusion(f32[3,64,64,64]{3,2,1,0:T(8,128)} %get-tuple-element.93, f32[3,64,64,64]{3,2,1,0:T(8,128)} %get-tuple-element.94), kind=kLoop, calls=%fused_computation.91 | loop fusion | flops 14942208 | bytes 12582912 | tf_op jit(solution)/shard_map/while/body/eval_jaxpr/vmap()/add | solution.py:103
  271.9 43.3 %multiply_reduce_fusion = (f32[64,64,64]{2,1,0:T(8,128)}, f32[3,64,64,64]{3,2,1,0:T(8,128)}) fusion(f32[3,64,64,64]{3,2,1,0:T(8,128)} %get-tuple-element.30, f32[3,64,64,64]{3,2,1,0:T(8,128)} %get-tuple-element.92, f32[3,64,64,64]{3,2,1,0:T(8,128)} %get-tuple-element.91, f32[3,64,64,64]{3,2,1,0:T(8,128)} %get-tuple-element.93, f32[64,64,64]{2,1,0:T(8,128)S(1)} %mul.165), kind=kLoop, calls=%fused_computation.90 | loop fusion | flops 20185088 | bytes 17825792 | tf_op jit(solution)/shard_map/while/body/eval_jaxpr/reduce_sum | solution.py:123
  315.2 6.9 %broadcast_multiply_fusion = f32[3,64,64,64]{3,2,1,0:T(8,128)} fusion(f32[3,64,64,64]{3,2,1,0:T(8,128)} %get-tuple-element.90, f32[64,64,64]{2,1,0:T(8,128)S(1)} %mul.165), kind=kLoop, calls=%fused_computation.95 | loop fusion | flops 786432 | bytes 7340032 | tf_op jit(solution)/shard_map/while/body/eval_jaxpr/vmap()/mul | solution.py:120
  322.1 10.5 %pad.55 = f32[3,96,96,96]{3,2,1,0:T(8,128)} pad(f32[3,64,64,64]{3,2,1,0:T(8,128)} %broadcast_multiply_fusion, f32[]{:T(128)} %constant.178.clone.1), padding=0_0x16_16x16_16x16_16 | pad | bytes 13762564 | tf_op jit(solution)/shard_map/while/body/eval_jaxpr/vmap(jit(_pad))/pad | solution.py:110
  332.6 3.4 broadcast.168
  335.9 20.1 %while.3 = (s32[]{:T(128)}, f32[3,96,96,96]{3,2,1,0:T(8,128)}, s32[3,4]{1,0:T(4,128)S(1)}, f32[3,64,64,64]{3,2,1,0:T(8,128)}, s32[]{:T(128)}) while((s32[]{:T(128)}, f32[3,96,96,96]{3,2,1,0:T(8,128)}, s32[3,4]{1,0:T(4,128)S(1)}, f32[3,64,64,64]{3,2,1,0:T(8,128)}, s32[]{:T(128)}) %tuple.78), condition=%wide.while_cond.1, body=%wide.while_body.1.sunk | while | flops 2 | bytes 4196993 | solution.py:112
  335.9 0.6 fusion.86
  336.6 6.1 %dynamic-slice_dynamic-update-slice_fusion.5 = f32[3,64,64,64]{3,2,1,0:T(8,128)} fusion(f32[3,64,64,64]{3,2,1,0:T(8,128)} %get-tuple-element.219, s32[]{:T(128)} %get-tuple-element.216, f32[3,96,96,96]{3,2,1,0:T(8,128)} %get-tuple-element.222, s32[]{:T(128)} %bitcast.100, s32[]{:T(128)} %bitcast.101, s32[]{:T(128)} %bitcast.102, s32[]{:T(128)} %bitcast.103), kind=kLoop, calls=%fused_computation.4.clone.1 | loop fusion | bytes 4196864 | tf_op jit(solution)/shard_map/while/body/eval_jaxpr/vmap()/gather
  343.3 6.1 %dynamic-slice_dynamic-update-slice_fusion.5 = f32[3,64,64,64]{3,2,1,0:T(8,128)} fusion(f32[3,64,64,64]{3,2,1,0:T(8,128)} %get-tuple-element.219, s32[]{:T(128)} %get-tuple-element.216, f32[3,96,96,96]{3,2,1,0:T(8,128)} %get-tuple-element.222, s32[]{:T(128)} %bitcast.100, s32[]{:T(128)} %bitcast.101, s32[]{:T(128)} %bitcast.102, s32[]{:T(128)} %bitcast.103), kind=kLoop, calls=%fused_computation.4.clone.1 | loop fusion | bytes 4196864 | tf_op jit(solution)/shard_map/while/body/eval_jaxpr/vmap()/gather
  350.0 6.0 %dynamic-slice_dynamic-update-slice_fusion.5 = f32[3,64,64,64]{3,2,1,0:T(8,128)} fusion(f32[3,64,64,64]{3,2,1,0:T(8,128)} %get-tuple-element.219, s32[]{:T(128)} %get-tuple-element.216, f32[3,96,96,96]{3,2,1,0:T(8,128)} %get-tuple-element.222, s32[]{:T(128)} %bitcast.100, s32[]{:T(128)} %bitcast.101, s32[]{:T(128)} %bitcast.102, s32[]{:T(128)} %bitcast.103), kind=kLoop, calls=%fused_computation.4.clone.1 | loop fusion | bytes 4196864 | tf_op jit(solution)/shard_map/while/body/eval_jaxpr/vmap()/gather
  356.1 5.4 broadcast_in_dim.31
  361.4 12.0 %scatter_fusion = f32[5,64,64,64]{3,2,1,0:T(8,128)} fusion(f32[5,64,64,64]{3,2,1,0:T(8,128)} %broadcast_in_dim.31, s32[3]{0:T(128)S(1)} %fusion.74, f32[3,64,64,64]{3,2,1,0:T(8,128)} %get-tuple-element.38), kind=kCustom, calls=%fused_computation.1 | custom fusion | flops 786432 | bytes 9437196 | tf_op jit(solution)/shard_map/scatter-add | solution.py:178
  373.4 8.5 %slice.400 = f32[4,64,64,64]{3,2,1,0:T(8,128)} slice(f32[5,64,64,64]{3,2,1,0:T(8,128)} %scatter_fusion), slice={[1:5], [0:64], [0:64], [0:64]} | slice | bytes 8388608 | tf_op jit(solution)/shard_map/slice | solution.py:181
  381.9 2.0 slice_add_fusion
  383.9 1.3 concatenate.26
  385.2 7.3 %concatenate.27 = f32[4,8,256,128]{3,2,1,0:T(8,128)} reshape(f32[4,64,64,64]{3,2,1,0:T(8,128)} %slice.400) | data formatting | bytes 8388608 | tf_op jit(solution)/shard_map/concatenate | solution.py:181
  392.6 5.2 maximum_multiply_fusion
  397.8 2.2 dynamic-slice_bitcast_fusion
  400.0 1.6 collective-permute-start.1
  401.5 2.1 collective-permute-start.2
  404.0 2.3 collective-permute-start.3
  406.3 1.7 collective-permute-start.5
  408.1 7.8 %collective-permute-done.1 = f32[1,5,256,128]{3,2,0,1:T(8,128)} collective-permute-done((f32[1,5,256,128]{3,2,0,1:T(8,128)}, f32[1,5,256,128]{3,2,0,1:T(8,128)}, u32[]{:S(2)}, u32[]{:S(2)}) %collective-permute-start.1) | collective-permute-done | bytes 655392 | tf_op jit(solution)/shard_map/ppermute | solution.py:36
  416.2 3.9 fusion.56
  420.1 3.4 reshape.88
  423.6 10.3 %all-to-all-start.1 = ((f32[1,2048,128]{2,0,1:T(1,128)}), f32[1,2048,128]{2,0,1:T(1,128)}, u32[]{:S(2)}, u32[]{:S(2)}) async-start(f32[1,2048,128]{2,0,1:T(1,128)} %reshape.88), calls=%async_computation.1 | async-start | bytes 2097152 | tf_op jit(solution)/shard_map/all_to_all | solution.py:185
  434.3 2.0 constant_dynamic-update-slice_fusion.8
  436.4 2.0 constant_dynamic-update-slice_fusion.7
  438.3 73.0 %collective-permute-done.3 = f32[1,5,256,128]{3,2,0,1:T(8,128)} collective-permute-done((f32[1,5,256,128]{3,2,0,1:T(8,128)}, f32[1,5,256,128]{3,2,0,1:T(8,128)}, u32[]{:S(2)}, u32[]{:S(2)}) %collective-permute-start.3) | collective-permute-done | bytes 655392 | tf_op jit(solution)/shard_map/ppermute | solution.py:36
  511.3 2.0 constant_dynamic-update-slice_fusion.6
  513.3 12.1 %collective-permute-done.4 = f32[1,5,256,128]{3,2,0,1:T(8,128)} collective-permute-done((f32[1,5,256,128]{3,2,0,1:T(8,128)}, f32[1,5,256,128]{3,2,0,1:T(8,128)}, u32[]{:S(2)}, u32[]{:S(2)}) %collective-permute-start.4) | collective-permute-done | bytes 655392 | tf_op jit(solution)/shard_map/ppermute | solution.py:36
  525.4 2.0 constant_dynamic-update-slice_fusion.5
  527.4 0.9 constant_dynamic-update-slice_fusion.4
  528.3 2.1 collective-permute-done.6
  530.4 0.9 constant_dynamic-update-slice_fusion.3
  531.3 10.7 %collective-permute-done.7 = f32[1,5,256,128]{3,2,0,1:T(8,128)S(1)} collective-permute-done((f32[1,5,256,128]{3,2,0,1:T(8,128)}, f32[1,5,256,128]{3,2,0,1:T(8,128)S(1)}, u32[]{:S(2)}, u32[]{:S(2)}) %collective-permute-start.7) | collective-permute-done | bytes 655392 | tf_op jit(solution)/shard_map/ppermute | solution.py:36
  542.1 0.9 constant_dynamic-update-slice_fusion.2
  543.0 3.0 fusion.82
  546.1 1.8 collective-permute-start.8
  548.2 7.4 %collective-permute-done.8 = f32[4,256,128]{2,1,0:T(8,128)S(1)} collective-permute-done((f32[4,256,128]{2,1,0:T(8,128)S(1)}, f32[4,256,128]{2,1,0:T(8,128)S(1)}, u32[]{:S(2)}, u32[]{:S(2)}) %collective-permute-start.8) | collective-permute-done | bytes 524320 | tf_op jit(solution)/shard_map/ppermute | solution.py:43
  555.5 3.5 multiply_add_fusion.2
  (44 shorter events, 4.0 us)
Async XLA Ops:
  1.7 12.9 %collective-permute-start = (f32[4,256,128]{2,1,0:T(8,128)S(1)}, f32[4,256,128]{2,1,0:T(8,128)S(1)}, u32[]{:S(2)}, u32[]{:S(2)}) collective-permute-start(f32[4,256,128]{2,1,0:T(8,128)S(1)} %slice.280), channel_id=1, source_target_pairs={{0,24},{8,0},{16,8},{24,16},{1,25},{9,1},{17,9},{25,17},{2,26},{10... | collective-permute-start | bytes 1572872 | tf_op jit(solution)/shard_map/ppermute | solution.py:43
  14.8 8.9 %copy-start.4 = (s32[1,3,3]{2,0,1:T(1,128)S(1)}, s32[1,3,3]{2,0,1:T(1,128)}, u32[]{:S(2)}) copy-start(s32[1,3,3]{2,0,1:T(1,128)} %param.9) | copy-start | bytes 112
  14.9 9.4 %copy-start.5 = (s32[1,3]{1,0:T(1,128)S(1)}, s32[1,3]{1,0:T(1,128)}, u32[]{:S(2)}) copy-start(s32[1,3]{1,0:T(1,128)} %param.8) | copy-start | bytes 40
  14.9 2.4 copy-start.2
  17.3 119.4 %all-to-all-start = ((f32[40,256,128]{2,1,0:T(8,128)}), f32[40,256,128]{2,1,0:T(8,128)}, u32[]{:S(2)}, u32[]{:S(2)}) async-start(f32[40,256,128]{2,1,0:T(8,128)} %bitcast.104), calls=%async_computation | async-start | bytes 10485760 | tf_op jit(solution)/shard_map/all_to_all | solution.py:163
  373.4 8.5 %copy-start.1 = (f32[64,64,64]{2,1,0:T(8,128)S(1)}, f32[64,64,64]{2,1,0:T(8,128)}, u32[]{:S(2)}) copy-start(f32[64,64,64]{2,1,0:T(8,128)} %get-tuple-element.89) | copy-start | bytes 3145732
  385.2 7.3 %copy-start.3 = (f32[1,8,256,128]{3,2,1,0:T(8,128)S(1)}, f32[1,8,256,128]{3,2,1,0:T(8,128)}, u32[]{:S(2)}) copy-start(f32[1,8,256,128]{3,2,1,0:T(8,128)} %concatenate.26) | copy-start | bytes 3145732
  400.0 15.9 %collective-permute-start.1 = (f32[1,5,256,128]{3,2,0,1:T(8,128)}, f32[1,5,256,128]{3,2,0,1:T(8,128)}, u32[]{:S(2)}, u32[]{:S(2)}) collective-permute-start(f32[1,5,256,128]{3,2,0,1:T(8,128)} %get-tuple-element.114), channel_id=1, source_target_pairs={{0,1},{1,2},{2,3},{3,4},{4,5},{5,6},{6,7},{7,0},{8,9},{9,10},{10,1... | collective-permute-start | bytes 1966088 | tf_op jit(solution)/shard_map/ppermute | solution.py:36
  401.5 32.3 %collective-permute-start.2 = (f32[1,5,256,128]{3,2,0,1:T(8,128)}, f32[1,5,256,128]{3,2,0,1:T(8,128)}, u32[]{:S(2)}, u32[]{:S(2)}) collective-permute-start(f32[1,5,256,128]{3,2,0,1:T(8,128)} %get-tuple-element.113), channel_id=1, source_target_pairs={{0,2},{1,3},{2,4},{3,5},{4,6},{5,7},{6,0},{7,1},{8,10},{9,11},{10,... | collective-permute-start | bytes 1966088 | tf_op jit(solution)/shard_map/ppermute | solution.py:36
  404.0 107.3 %collective-permute-start.3 = (f32[1,5,256,128]{3,2,0,1:T(8,128)}, f32[1,5,256,128]{3,2,0,1:T(8,128)}, u32[]{:S(2)}, u32[]{:S(2)}) collective-permute-start(f32[1,5,256,128]{3,2,0,1:T(8,128)} %get-tuple-element.112), channel_id=1, source_target_pairs={{0,3},{1,4},{2,5},{3,6},{4,7},{5,0},{6,1},{7,2},{8,11},{9,12},{10,... | collective-permute-start | bytes 1966088 | tf_op jit(solution)/shard_map/ppermute | solution.py:36
  406.3 119.1 %collective-permute-start.4 = (f32[1,5,256,128]{3,2,0,1:T(8,128)}, f32[1,5,256,128]{3,2,0,1:T(8,128)}, u32[]{:S(2)}, u32[]{:S(2)}) collective-permute-start(f32[1,5,256,128]{3,2,0,1:T(8,128)} %get-tuple-element.111), channel_id=1, source_target_pairs={{0,4},{1,5},{2,6},{3,7},{4,0},{5,1},{6,2},{7,3},{8,12},{9,13},{10,... | collective-permute-start | bytes 1966088 | tf_op jit(solution)/shard_map/ppermute | solution.py:36
  406.3 121.1 %collective-permute-start.5 = (f32[1,5,256,128]{3,2,0,1:T(8,128)}, f32[1,5,256,128]{3,2,0,1:T(8,128)S(1)}, u32[]{:S(2)}, u32[]{:S(2)}) collective-permute-start(f32[1,5,256,128]{3,2,0,1:T(8,128)} %get-tuple-element.110), channel_id=1, source_target_pairs={{0,5},{1,6},{2,7},{3,0},{4,1},{5,2},{6,3},{7,4},{8,13},{9,14},{10,... | collective-permute-start | bytes 1966088 | tf_op jit(solution)/shard_map/ppermute | solution.py:36
  415.8 114.6 %collective-permute-start.6 = (f32[1,5,256,128]{3,2,0,1:T(8,128)}, f32[1,5,256,128]{3,2,0,1:T(8,128)S(1)}, u32[]{:S(2)}, u32[]{:S(2)}) collective-permute-start(f32[1,5,256,128]{3,2,0,1:T(8,128)} %get-tuple-element.109), channel_id=1, source_target_pairs={{0,6},{1,7},{2,0},{3,1},{4,2},{5,3},{6,4},{7,5},{8,14},{9,15},{10,... | collective-permute-start | bytes 1966088 | tf_op jit(solution)/shard_map/ppermute | solution.py:36
  423.6 132.0 %all-to-all-start.1 = ((f32[1,2048,128]{2,0,1:T(1,128)}), f32[1,2048,128]{2,0,1:T(1,128)}, u32[]{:S(2)}, u32[]{:S(2)}) async-start(f32[1,2048,128]{2,0,1:T(1,128)} %reshape.88), calls=%async_computation.1 | async-start | bytes 2097152 | tf_op jit(solution)/shard_map/all_to_all | solution.py:185
  433.8 108.2 %collective-permute-start.7 = (f32[1,5,256,128]{3,2,0,1:T(8,128)}, f32[1,5,256,128]{3,2,0,1:T(8,128)S(1)}, u32[]{:S(2)}, u32[]{:S(2)}) collective-permute-start(f32[1,5,256,128]{3,2,0,1:T(8,128)} %get-tuple-element.108), channel_id=1, source_target_pairs={{0,7},{1,0},{2,1},{3,2},{4,3},{5,4},{6,5},{7,6},{8,15},{9,8},{10,9... | collective-permute-start | bytes 1966088 | tf_op jit(solution)/shard_map/ppermute | solution.py:36
  546.0 9.5 %copy-start = (f32[8,256,128]{2,1,0:T(8,128)S(1)}, f32[8,256,128]{2,1,0:T(8,128)}, u32[]{:S(2)}) copy-start(f32[8,256,128]{2,1,0:T(8,128)} %param.5) | copy-start | bytes 3145732
  546.1 9.4 %collective-permute-start.8 = (f32[4,256,128]{2,1,0:T(8,128)S(1)}, f32[4,256,128]{2,1,0:T(8,128)S(1)}, u32[]{:S(2)}, u32[]{:S(2)}) collective-permute-start(f32[4,256,128]{2,1,0:T(8,128)S(1)} %add_bitcast_fusion), channel_id=1, source_target_pairs={{0,8},{8,16},{16,24},{24,0},{1,9},{9,17},{17,25},{25,1},{2,10},{10... | collective-permute-start | bytes 1572872 | tf_op jit(solution)/shard_map/ppermute | solution.py:43
